TPU v7x, 256 devices: a whole 4x4x8 slice. The times are simulated.
256 devices in a mesh: wide: 64 (over y, z, core), narrow: 4 (over x).
Axes of the slice: x: 4, y: 4, z: 8, core: 2. Of those that a mesh axis runs over, the one named last changes fastest.
Arguments:
- patches: bfloat16 [65536, 1280], P('wide', 'narrow'), may hold values from -6 to 6
- norm_gain: float32 [1280], replicated, may hold values from 0.1 to 1.9
- norm_bias: float32 [1280], replicated, may hold values from -3 to 3
- w_in: bfloat16 [1280, 5120], P('wide', 'narrow'), may hold values from -0.15625 to 0.15625
- b_in: float32 [5120], P('narrow'), may hold values from -3 to 3
- w_out: bfloat16 [5120, 1280], P('narrow', 'wide'), may hold values from -0.078125 to 0.078125
- b_out: float32 [1280], P('narrow'), may hold values from -3 to 3
- w_proj: bfloat16 [4, 1280, 1280], P(None, 'narrow', 'wide'), may hold values from -0.078125 to 0.078125
- b_proj: float32 [1280], P('narrow'), may hold values from -3 to 3
- text: bfloat16 [32768, 1280], P('wide', 'narrow'), may hold values from -6 to 6
- place: int32 [16384], replicated, may hold values from -1 to 32767, as said below
Outputs:
- prompt_embeds: bfloat16 [32768, 1280], P('wide', 'narrow')
Inputs may be any that keep to these rules, and one draw needn't show every extreme that they name: `place`: of the 256 entries of one wide index (entries i * 256 to (i + 1) * 256 - 1), the valid ones (>= 0) come first and -1 fills the rest; three quarters or more are valid, and all are valid for some wide index. Valid values are distinct. For one wide index, at most 8 valid entries v have the same v // 512, and every wide index reaches 8 for some value.
All inputs are finite; a program needn't handle non-finite values.
Results may differ from a plain program's by a relative error of at most 0.012.
Values may be sent and summed in bfloat16 or wider, within the bound.
A program may use at most 64 MiB of HBM per device.

v0:
```python
import jax
import jax.numpy as jnp
from jax import lax
from jax.sharding import PartitionSpec as P


def per_device(
    patches, norm_gain, norm_bias, w_in, b_in, w_out, b_out, w_proj, b_proj, text, place
):
    whole = lax.all_gather(patches, "narrow", axis=1, tiled=True)
    values = whole.astype(jnp.float32)
    center = jnp.mean(values, axis=-1, keepdims=True)
    spread = jnp.mean(jnp.square(values - center), axis=-1, keepdims=True)
    normed = ((values - center) * lax.rsqrt(spread + 1e-06) * norm_gain + norm_bias).astype(
        jnp.bfloat16
    )
    rows_in, cols_out, proj_cols = (
        lax.all_gather(w_in, "wide", axis=0, tiled=True),
        lax.all_gather(w_out, "wide", axis=1, tiled=True),
        lax.all_gather(w_proj, "wide", axis=2, tiled=True),
    )
    product = jnp.dot(normed, rows_in, preferred_element_type=jnp.float32)
    hidden = jax.nn.gelu(product + b_in, approximate=False).astype(jnp.bfloat16)
    partial_out = jnp.dot(hidden, cols_out, preferred_element_type=jnp.float32)
    mlp_out = lax.psum_scatter(
        partial_out.astype(jnp.bfloat16), "narrow", scatter_dimension=1, tiled=True
    ).astype(jnp.float32)
    stream = (patches.astype(jnp.float32) + (mlp_out + b_out)).astype(jnp.bfloat16)
    merge_count = stream.shape[0] // 4
    merged = stream.reshape(merge_count, 4 * stream.shape[1])
    groups = lax.axis_size("wide")
    own_index = lax.axis_index("wide")
    seq_rows = text.shape[0]
    bucket = seq_rows // groups
    place_table = place.reshape(groups, merge_count)
    owners = jnp.where(place_table >= 0, place_table // seq_rows, groups)
    own_owners = lax.dynamic_index_in_dim(owners, own_index, 0, keepdims=False)
    owner_hits = (own_owners[:, None] == jnp.arange(groups, dtype=jnp.int32)[None, :]).astype(
        jnp.int32
    )
    slot_out = jnp.sum(jnp.cumsum(owner_hits, axis=0) * owner_hits, axis=1) - 1
    slot_out = jnp.where(own_owners < groups, slot_out, bucket)
    arriving = owners == own_index
    slot_in = jnp.cumsum(arriving.astype(jnp.int32), axis=1) - 1
    slot_in = jnp.where(arriving, slot_in, bucket)
    local_row = jnp.where(arriving, place_table % seq_rows, seq_rows)
    source_ids = jnp.arange(groups, dtype=jnp.int32)[:, None]
    targets = (
        jnp.full((groups, bucket), seq_rows, jnp.int32)
        .at[source_ids, slot_in]
        .set(local_row, mode="drop")
    )
    partial_proj = jnp.dot(
        merged, proj_cols.reshape(-1, proj_cols.shape[2]), preferred_element_type=jnp.float32
    )
    vision = (
        lax.psum_scatter(
            partial_proj.astype(jnp.bfloat16), "narrow", scatter_dimension=1, tiled=True
        ).astype(jnp.float32)
        + b_proj
    ).astype(jnp.bfloat16)
    buffer = jnp.zeros((groups, bucket, vision.shape[1]), vision.dtype)
    received = lax.all_to_all(
        buffer.at[own_owners, slot_out].set(vision, mode="drop"),
        "wide",
        split_axis=0,
        concat_axis=0,
        tiled=True,
    )
    return text.at[targets.reshape(-1)].set(received.reshape(-1, received.shape[2]), mode="drop")


def solution(mesh):
    placed = (
        P("wide", "narrow"),
        P(),
        P(),
        P("wide", "narrow"),
        P("narrow"),
        P("narrow", "wide"),
        P("narrow"),
        P(None, "narrow", "wide"),
        P("narrow"),
        P("wide", "narrow"),
        P(),
    )
    return jax.shard_map(
        per_device, mesh=mesh, in_specs=placed, out_specs=P("wide", "narrow"), check_vma=False
    )
```

profile of v0, /device:TPU:1, one launch (start us, length us, event | category | flops | bytes accessed | tf_op | source)
XLA Modules:
  0.0 475.5 jit_solution(18074952579770676036)
XLA Ops:
  6.5 0.7 all-gather.7.cloned.1.call-update
  7.3 0.7 all-gather.13.cloned.1.call-update
  8.1 0.7 all-gather.11.cloned.1.call-update
  8.8 0.5 all-gather.9.cloned.1.call-update
  9.4 41.4 %all-gather.7.cloned.1.call-done = bf16[1024,1280]{0,1:T(8,128)(2,1)} async-done(((bf16[1024,320]{0,1:T(8,128)(2,1)}), bf16[1024,1280]{0,1:T(8,128)(2,1)}) %all-gather.7.cloned.1.call-update) | async-done | bytes 2621456 | tf_op jit(solution)/shard_map/all_gather | solution.py:10
  50.7 2.3 convert_reduce_fusion
  53.2 0.7 fusion.2
  54.0 78.9 %all-gather.13.cloned.1.call-done = bf16[64,20,1280]{2,1,0:T(8,128)(2,1)} async-done(((bf16[1,20,1280]{2,1,0:T(8,128)(2,1)}), bf16[64,20,1280]{2,1,0:T(8,128)(2,1)}) %all-gather.13.cloned.1.call-update) | async-done | bytes 3276816 | tf_op jit(solution)/shard_map/all_gather | solution.py:19
  132.9 6.1 %reshape.317 = bf16[1280,1280]{1,0:T(8,128)(2,1)} reshape(bf16[64,20,1280]{2,1,0:T(8,128)(2,1)} %all-gather.13.cloned.1.call-done) | data formatting | bytes 6553600
  139.1 72.6 %all-gather.11.cloned.1.call-done = bf16[64,20,1280]{2,1,0:T(8,128)(2,1)} async-done(((bf16[1,20,1280]{2,1,0:T(8,128)(2,1)}), bf16[64,20,1280]{2,1,0:T(8,128)(2,1)}) %all-gather.11.cloned.1.call-update) | async-done | bytes 3276816 | tf_op jit(solution)/shard_map/all_gather | solution.py:18
  211.7 6.1 %reshape.315 = bf16[1280,1280]{1,0:T(8,128)(2,1)} reshape(bf16[64,20,1280]{2,1,0:T(8,128)(2,1)} %all-gather.11.cloned.1.call-done) | data formatting | bytes 6553600
  217.8 21.4 %convolution_convert_fusion = bf16[1024,1280]{0,1:T(8,128)(2,1)} fusion(bf16[1280,1280]{1,0:T(8,128)(2,1)} %reshape.317, bf16[1280,1280]{1,0:T(8,128)(2,1)} %reshape.315, bf16[1024,1280]{0,1:T(8,128)(2,1)S(1)} %copy-done, f32[1280]{0:T(1024)S(1)} %copy-done.6, f32[1280]{0:T(1024)S(1)} %copy-done.7, f32[1280]{0:T(1024)S(1)} %copy-done.8, ...), kind=kOutput, calls=%fused_computation.30 | convolution fusion | flops 6806568960 | bytes 11820032 | tf_op jit(solution)/shard_map/dot_general | solution.py:24
  239.4 0.6 reduce-window.14
  240.0 0.2 slice_reduce_fusion.1
  240.4 49.9 %all-gather.9.cloned.1.call-done = bf16[4,320,1280]{1,0,2:T(4,128)(2,1)} async-done(((bf16[4,320,20]{1,0,2:T(4,128)(2,1)}), bf16[4,320,1280]{1,0,2:T(4,128)(2,1)}) %all-gather.9.cloned.1.call-update) | async-done | bytes 3276816 | tf_op jit(solution)/shard_map/all_gather | solution.py:20
  290.3 7.3 %copy.46 = bf16[4,320,1280]{2,1,0:T(8,128)(2,1)S(1)} copy(bf16[4,320,1280]{1,0,2:T(4,128)(2,1)} %all-gather.9.cloned.1.call-done) | data formatting | bytes 6553600 | tf_op jit(solution)/shard_map/all_gather | solution.py:20
  297.6 28.3 %reduce-scatter.3.cloned.1.call-done = bf16[1024,320]{0,1:T(8,128)(2,1)} async-done(((bf16[1024,1280]{0,1:T(8,128)(2,1)}), bf16[1024,320]{0,1:T(8,128)(2,1)}) %reduce-scatter.3.cloned.1.call-update) | async-done | bytes 655376 | tf_op jit(solution)/shard_map/reduce_scatter | solution.py:25
  326.0 2.4 add_convert_fusion
  328.4 2.2 copy.45
  330.6 2.5 reshape.287
  333.1 3.3 convolution_convert_fusion.1
  336.5 1.2 copy.48
  337.9 0.6 reduce-window.16
  338.5 0.2 slice_reduce_fusion
  338.9 20.6 %reduce-scatter.5.cloned.1.call-done = bf16[256,320]{0,1:T(8,128)(2,1)} async-done(((bf16[256,1280]{0,1:T(8,128)(2,1)}), bf16[256,320]{0,1:T(8,128)(2,1)}) %reduce-scatter.5.cloned.1.call-update) | async-done | bytes 163856 | tf_op jit(solution)/shard_map/reduce_scatter | solution.py:57
  359.5 1.0 add_convert_fusion.1
  360.7 0.8 broadcast_in_dim.47
  361.5 30.9 %scatter_fusion = bf16[64,8,320]{2,1,0:T(8,128)(2,1)} fusion(bf16[64,8,320]{2,1,0:T(8,128)(2,1)} %broadcast_in_dim.47, s32[256]{0:T(256)S(1)} %bitcast.42, bf16[256,320]{1,0:T(8,128)(2,1)S(1)} %copy.47), kind=kCustom, calls=%fused_computation | custom fusion | bytes 493568 | tf_op jit(solution)/shard_map/scatter | solution.py:64
  392.4 11.9 %all-to-all-start = ((bf16[64,8,320]{2,1,0:T(8,128)(2,1)}), bf16[64,8,320]{2,1,0:T(8,128)(2,1)S(1)}, u32[]{:S(2)}, u32[]{:S(2)}) async-start(bf16[64,8,320]{2,1,0:T(8,128)(2,1)} %scatter_fusion), calls=%async_computation.2 | async-start | bytes 786432 | tf_op jit(solution)/shard_map/all_to_all | solution.py:63
  404.6 60.3 %scatter_custom_fusion.2 = s32[512]{0:T(512)S(1)} fusion(s32[16384]{0:T(1024)S(1)} %bitcast.45, s32[16384]{0:T(1024)S(1)} %bitcast.46, s32[]{:T(128)} %constant.43.clone.1), kind=kCustom, calls=%fused_computation.95 | custom fusion | bytes 2052
  465.2 2.6 scatter_custom_fusion.1
  467.7 0.9 copy.49
  (57 shorter events, 1.8 us)
Async XLA Ops:
  6.5 44.2 %all-gather.7.cloned.1.call-start = ((), (), s32[]{:S(2)}) async-start(), calls=%async_computation.3 | async-start | bytes 3276800 | tf_op jit(solution)/shard_map/all_gather | solution.py:10
  7.3 125.7 %all-gather.13.cloned.1.call-start = ((), (), s32[]{:S(2)}) async-start(), calls=%async_computation.8 | async-start | bytes 3993600 | tf_op jit(solution)/shard_map/all_gather | solution.py:19
  8.0 203.7 %all-gather.11.cloned.1.call-start = ((), (), s32[]{:S(2)}) async-start(), calls=%async_computation.7 | async-start | bytes 3993600 | tf_op jit(solution)/shard_map/all_gather | solution.py:18
  8.7 281.6 %all-gather.9.cloned.1.call-start = ((), (), s32[]{:S(2)}) async-start(), calls=%async_computation.5 | async-start | bytes 3993600 | tf_op jit(solution)/shard_map/all_gather | solution.py:20
  9.3 316.6 %reduce-scatter.3.cloned.1.call-start = ((), (), s32[]{:S(2)}) async-start(), calls=%async_computation.4 | async-start | bytes 3276800 | tf_op jit(solution)/shard_map/reduce_scatter | solution.py:25
  50.7 2.5 copy-start
  139.1 78.8 %copy-start.6 = (f32[1280]{0:T(1024)S(1)}, f32[1280]{0:T(1024)}, u32[]{:S(2)}) copy-start(f32[1280]{0:T(1024)} %param.15) | copy-start | bytes 15364
  139.1 78.8 %copy-start.7 = (f32[1280]{0:T(1024)S(1)}, f32[1280]{0:T(1024)}, u32[]{:S(2)}) copy-start(f32[1280]{0:T(1024)} %param.13) | copy-start | bytes 15364
  139.1 78.8 %copy-start.8 = (f32[1280]{0:T(1024)S(1)}, f32[1280]{0:T(1024)}, u32[]{:S(2)}) copy-start(f32[1280]{0:T(1024)} %param.12) | copy-start | bytes 15364
  217.8 21.5 %copy-start.1 = (s32[16384]{0:T(1024)S(1)}, s32[16384]{0:T(1024)}, u32[]{:S(2)}) copy-start(s32[16384]{0:T(1024)} %param.21) | copy-start | bytes 196612
  239.2 86.7 %copy-start.2 = (f32[320]{0:T(512)S(1)}, f32[320]{0:T(512)}, u32[]{:S(2)}) copy-start(f32[320]{0:T(512)} %param.17) | copy-start | bytes 3844
  239.3 120.2 %reduce-scatter.5.cloned.1.call-start = ((), (), s32[]{:S(2)}) async-start(), calls=%async_computation.6 | async-start | bytes 819200 | tf_op jit(solution)/shard_map/reduce_scatter | solution.py:57
  333.1 26.4 %copy-start.3 = (f32[320]{0:T(512)S(1)}, f32[320]{0:T(512)}, u32[]{:S(2)}) copy-start(f32[320]{0:T(512)} %param.19) | copy-start | bytes 3844
  336.4 67.9 %copy-start.5 = (s32[2]{0:T(128)S(1)}, s32[2]{0:T(128)}, u32[]{:S(2)}) copy-start(s32[2]{0:T(128)} %constant.137) | copy-start | bytes 28
  336.4 68.0 %copy-start.4 = (s32[2]{0:T(128)S(1)}, s32[2]{0:T(128)}, u32[]{:S(2)}) copy-start(s32[2]{0:T(128)} %constant.140) | copy-start | bytes 28
  392.4 72.8 %all-to-all-start = ((bf16[64,8,320]{2,1,0:T(8,128)(2,1)}), bf16[64,8,320]{2,1,0:T(8,128)(2,1)S(1)}, u32[]{:S(2)}, u32[]{:S(2)}) async-start(bf16[64,8,320]{2,1,0:T(8,128)(2,1)} %scatter_fusion), calls=%async_computation.2 | async-start | bytes 786432 | tf_op jit(solution)/shard_map/all_to_all | solution.py:63
Sparse Core Ops, SparseCore 0:
  9.2 41.5 all-gather.6
  53.4 79.4 all-gather.12
  135.6 76.0 all-gather.10
  214.3 75.9 all-gather.8
  292.7 33.2 reduce-scatter.2
  336.5 22.9 reduce-scatter.4
where the time goes:
time: 477 us; the launch traced here: 475 us
  waiting for transfers between devices  294 us (62%)
  local copies, waits for them, and re-layouts  122 us (26%)
  matrix products  24.7 us (5%)
  between operations  13.7 us (3%)
  starting transfers between devices  12.1 us (3%)
  other arithmetic  8.4 us (2%)
    all_gather x1, waiting for transfers between devices, per_device(): lax.all_gather(w_out, 'wide', axis=1, tiled=True)  78.9 us
    unnamed x25, local copies, waits for them, and re-layouts  74.1 us
    all_gather x1, waiting for transfers between devices, per_device(): lax.all_gather(w_in, 'wide', axis=0, tiled=True)  72.6 us
    all_gather x1, waiting for transfers between devices, per_device(): lax.all_gather(w_proj, 'wide', axis=2, tiled=True)  49.9 us
    all_gather x1, waiting for transfers between devices, per_device(): whole = lax.all_gather(patches, 'narrow', axis=1, tiled=True)  41.4 us
    scatter x1, local copies, waits for them, and re-layouts, per_device(): buffer.at[own_owners, slot_out].set(vision, mode='drop')  30.9 us
    reduce_scatter x1, waiting for transfers between devices, per_device(): lax.psum_scatter(partial_out.astype(jnp.bfloat16), 'narrow', scatter_dime...  28.3 us
    dot_general x1, matrix products, per_device(): partial_out = jnp.dot(hidden, cols_out, preferred_element_type=jnp.float32)  21.4 us
  transfers between devices with their start and end apart: 7, of which 6 were waited for; matrix products, arithmetic and copies ran while one was open for 23% of the time, Pallas kernels for 0%

commit v1 on v0

--- a/solution.py
+++ b/solution.py
@@ -4,10 +4,20 @@
 from jax.sharding import PartitionSpec as P
 
 
+def turned_line(x, axis, dim):
+    devices = lax.axis_size(axis)
+    moving, blocks = (x, [x])
+    for _ in range(devices - 1):
+        moving = lax.ppermute(moving, axis, [(i, (i + 1) % devices) for i in range(devices)])
+        blocks.insert(0, moving)
+    line = jnp.concatenate(blocks, axis=dim)
+    return jnp.roll(line, (lax.axis_index(axis) + 1) * x.shape[dim], axis=dim)
+
+
 def per_device(
     patches, norm_gain, norm_bias, w_in, b_in, w_out, b_out, w_proj, b_proj, text, place
 ):
-    whole = lax.all_gather(patches, "narrow", axis=1, tiled=True)
+    whole = turned_line(patches, "narrow", 1)
     values = whole.astype(jnp.float32)
     center = jnp.mean(values, axis=-1, keepdims=True)
     spread = jnp.mean(jnp.square(values - center), axis=-1, keepdims=True)

time: 477 us -> 434 us (0.910)
  waiting for transfers between devices: 294 us -> 248 us
  starting transfers between devices: 12.1 us -> 17 us
    all_gather x1 -> x0, waiting for transfers between devices: 41.4 us -> none  [per_device(): whole = lax.all_gather(patches, 'narrow', axis=1, tiled=True)]
    ppermute x0 -> x3, waiting for transfers between devices: none -> 40.1 us  [turned_line(): lax.ppermute(moving, axis, [(i, (i + 1) % devices) for i in range(devices)])]
    all_gather x1, waiting for transfers between devices: 72.6 us -> 35.1 us  [per_device(): lax.all_gather(w_in, 'wide', axis=0, tiled=True)]
    all_gather x1, waiting for transfers between devices: 78.9 us -> 72.7 us  [per_device(): lax.all_gather(w_out, 'wide', axis=1, tiled=True)]
    ppermute x0 -> x3, starting transfers between devices: none -> 4.95 us  [turned_line(): lax.ppermute(moving, axis, [(i, (i + 1) % devices) for i in range(devices)])]
    unnamed x25 -> x38, local copies, waits for them, and re-layouts: 74.1 us -> 75.8 us
  transfers between devices with their start and end apart: 7 -> 9, of which waited for: 6 -> 8; matrix products, arithmetic and copies ran while one was open for 23% -> 25% of each run, Pallas kernels for 0% -> 0%
where the time goes in v1:
time: 434 us; the launch traced here: 432 us
  waiting for transfers between devices  248 us (57%)
  local copies, waits for them, and re-layouts  121 us (28%)
  matrix products  26.4 us (6%)
  starting transfers between devices  17 us (4%)
  between operations  13.6 us (3%)
  other arithmetic  6.12 us (1%)
    unnamed x38, local copies, waits for them, and re-layouts  75.8 us
    all_gather x1, waiting for transfers between devices, per_device(): lax.all_gather(w_out, 'wide', axis=1, tiled=True)  72.7 us
    all_gather x1, waiting for transfers between devices, per_device(): lax.all_gather(w_proj, 'wide', axis=2, tiled=True)  49.3 us
    ppermute x3, waiting for transfers between devices, turned_line(): lax.ppermute(moving, axis, [(i, (i + 1) % devices) for i in range(devices)])  40.1 us
    all_gather x1, waiting for transfers between devices, per_device(): lax.all_gather(w_in, 'wide', axis=0, tiled=True)  35.1 us
    scatter x1, local copies, waits for them, and re-layouts, per_device(): buffer.at[own_owners, slot_out].set(vision, mode='drop')  30.9 us
    reduce_scatter x1, waiting for transfers between devices, per_device(): lax.psum_scatter(partial_out.astype(jnp.bfloat16), 'narrow', scatter_dime...  27.9 us
    dot_general x1, matrix products, per_device(): partial_out = jnp.dot(hidden, cols_out, preferred_element_type=jnp.float32)  22.2 us
  transfers between devices with their start and end apart: 9, of which 8 were waited for; matrix products, arithmetic and copies ran while one was open for 25% of the time, Pallas kernels for 0%

profile of v1, /device:TPU:1, one launch (start us, length us, event | category | flops | bytes accessed | tf_op | source)
XLA Modules:
  0.0 432.0 jit_solution(1523848726433789980)
XLA Ops:
  6.5 0.7 all-gather.8.cloned.1.call-update
  7.3 0.7 all-gather.10.cloned.1.call-update
  8.1 2.1 collective-permute-start
  10.2 13.6 %collective-permute-done = bf16[1024,320]{0,1:T(8,128)(2,1)S(1)} collective-permute-done((bf16[1024,320]{0,1:T(8,128)(2,1)}, bf16[1024,320]{0,1:T(8,128)(2,1)S(1)}, u32[]{:S(2)}, u32[]{:S(2)}) %collective-permute-start) | collective-permute-done | bytes 655392 | tf_op jit(solution)/shard_map/ppermute | solution.py:11
  23.8 1.9 collective-permute-start.1
  25.7 13.6 %collective-permute-done.1 = bf16[1024,320]{0,1:T(8,128)(2,1)S(1)} collective-permute-done((bf16[1024,320]{0,1:T(8,128)(2,1)S(1)}, bf16[1024,320]{0,1:T(8,128)(2,1)S(1)}, u32[]{:S(2)}, u32[]{:S(2)}) %collective-permute-start.1) | collective-permute-done | bytes 655392 | tf_op jit(solution)/shard_map/ppermute | solution.py:11
  39.2 0.9 collective-permute-start.2
  40.3 12.9 %collective-permute-done.2 = bf16[1024,320]{0,1:T(8,128)(2,1)S(1)} collective-permute-done((bf16[1024,320]{0,1:T(8,128)(2,1)S(1)}, bf16[1024,320]{0,1:T(8,128)(2,1)S(1)}, u32[]{:S(2)}, u32[]{:S(2)}) %collective-permute-start.2) | collective-permute-done | bytes 655392 | tf_op jit(solution)/shard_map/ppermute | solution.py:11
  53.4 1.1 constant_dynamic-update-slice_fusion.4
  54.7 0.8 convert_reduce_fusion
  55.5 1.5 copy-done
  57.0 1.1 fusion.2
  58.1 35.1 %all-gather.8.cloned.1.call-done = bf16[64,20,1280]{2,1,0:T(8,128)(2,1)} async-done(((bf16[1,20,1280]{2,1,0:T(8,128)(2,1)}), bf16[64,20,1280]{2,1,0:T(8,128)(2,1)}) %all-gather.8.cloned.1.call-update) | async-done | bytes 3276816 | tf_op jit(solution)/shard_map/all_gather | solution.py:28
  93.2 6.1 %reshape.315 = bf16[1280,1280]{1,0:T(8,128)(2,1)} reshape(bf16[64,20,1280]{2,1,0:T(8,128)(2,1)} %all-gather.8.cloned.1.call-done) | data formatting | bytes 6553600
  99.3 72.7 %all-gather.10.cloned.1.call-done = bf16[64,20,1280]{2,1,0:T(8,128)(2,1)} async-done(((bf16[1,20,1280]{2,1,0:T(8,128)(2,1)}), bf16[64,20,1280]{2,1,0:T(8,128)(2,1)}) %all-gather.10.cloned.1.call-update) | async-done | bytes 3276816 | tf_op jit(solution)/shard_map/all_gather | solution.py:29
  172.0 6.1 %reshape.317 = bf16[1280,1280]{1,0:T(8,128)(2,1)} reshape(bf16[64,20,1280]{2,1,0:T(8,128)(2,1)} %all-gather.10.cloned.1.call-done) | data formatting | bytes 6553600
  178.1 22.2 %convolution_convert_fusion = bf16[1024,1280]{0,1:T(8,128)(2,1)} fusion(bf16[1280,1280]{1,0:T(8,128)(2,1)} %reshape.317, bf16[1280,1280]{1,0:T(8,128)(2,1)} %reshape.315, f32[1280]{0:T(1024)S(1)} %copy-done.9, f32[1280]{0:T(1024)S(1)} %copy-done.10, f32[1280]{0:T(1024)S(1)} %copy-done.11, f32[1024]{0:T(1024)S(1)} %add_rsqrt_fusion, ...), kind=kOutput, calls=%fused_computation.30 | convolution fusion | flops 6806568960 | bytes 11820036 | tf_op jit(solution)/shard_map/dot_general | solution.py:34
  200.6 0.6 reduce-window.16
  201.4 49.3 %all-gather.6.cloned.1.call-done = bf16[4,320,1280]{1,0,2:T(4,128)(2,1)} async-done(((bf16[4,320,20]{1,0,2:T(4,128)(2,1)}), bf16[4,320,1280]{1,0,2:T(4,128)(2,1)}) %all-gather.6.cloned.1.call-update) | async-done | bytes 3276816 | tf_op jit(solution)/shard_map/all_gather | solution.py:30
  250.7 7.8 %copy.46 = bf16[4,320,1280]{2,1,0:T(8,128)(2,1)} copy(bf16[4,320,1280]{1,0,2:T(4,128)(2,1)} %all-gather.6.cloned.1.call-done) | data formatting | bytes 6553600 | tf_op jit(solution)/shard_map/all_gather | solution.py:30
  258.5 27.9 %reduce-scatter.3.cloned.1.call-done = bf16[1024,320]{0,1:T(8,128)(2,1)} async-done(((bf16[1024,1280]{0,1:T(8,128)(2,1)}), bf16[1024,320]{0,1:T(8,128)(2,1)}) %reduce-scatter.3.cloned.1.call-update) | async-done | bytes 655376 | tf_op jit(solution)/shard_map/reduce_scatter | solution.py:35
  286.4 1.3 add_convert_fusion
  288.2 0.7 reshape.287
  288.9 4.2 convolution_convert_fusion.1
  294.4 21.7 %reduce-scatter.5.cloned.1.call-done = bf16[256,320]{0,1:T(8,128)(2,1)} async-done(((bf16[256,1280]{0,1:T(8,128)(2,1)}), bf16[256,320]{0,1:T(8,128)(2,1)}) %reduce-scatter.5.cloned.1.call-update) | async-done | bytes 163856 | tf_op jit(solution)/shard_map/reduce_scatter | solution.py:67
  316.1 1.0 add_convert_fusion.1
  317.3 0.8 broadcast_in_dim.47
  318.1 30.9 %scatter_fusion = bf16[64,8,320]{2,1,0:T(8,128)(2,1)} fusion(bf16[64,8,320]{2,1,0:T(8,128)(2,1)} %broadcast_in_dim.47, s32[256]{0:T(256)S(1)} %bitcast.42, bf16[256,320]{1,0:T(8,128)(2,1)S(1)} %copy.47), kind=kCustom, calls=%fused_computation | custom fusion | bytes 493568 | tf_op jit(solution)/shard_map/scatter | solution.py:74
  349.0 11.9 %all-to-all-start = ((bf16[64,8,320]{2,1,0:T(8,128)(2,1)}), bf16[64,8,320]{2,1,0:T(8,128)(2,1)S(1)}, u32[]{:S(2)}, u32[]{:S(2)}) async-start(bf16[64,8,320]{2,1,0:T(8,128)(2,1)} %scatter_fusion), calls=%async_computation.2 | async-start | bytes 786432 | tf_op jit(solution)/shard_map/all_to_all | solution.py:73
  361.2 60.3 %scatter_custom_fusion.2 = s32[512]{0:T(512)S(1)} fusion(s32[16384]{0:T(1024)S(1)} %bitcast.45, s32[16384]{0:T(1024)S(1)} %bitcast.46, s32[]{:T(128)} %constant.47.clone.1), kind=kCustom, calls=%fused_computation.104 | custom fusion | bytes 2052
  422.0 2.6 scatter_custom_fusion.1
  424.6 0.9 copy.49
  (75 shorter events, 3.5 us)
Async XLA Ops:
  6.5 48.1 %copy-start.1 = (bf16[1024,320]{0,1:T(8,128)(2,1)S(1)}, bf16[1024,320]{0,1:T(8,128)(2,1)}, u32[]{:S(2)}) copy-start(bf16[1024,320]{0,1:T(8,128)(2,1)} %param.11) | copy-start | bytes 1966084
  6.5 86.7 %all-gather.8.cloned.1.call-start = ((), (), s32[]{:S(2)}) async-start(), calls=%async_computation.6 | async-start | bytes 3993600 | tf_op jit(solution)/shard_map/all_gather | solution.py:28
  7.3 164.7 %all-gather.10.cloned.1.call-start = ((), (), s32[]{:S(2)}) async-start(), calls=%async_computation.7 | async-start | bytes 3993600 | tf_op jit(solution)/shard_map/all_gather | solution.py:29
  8.0 242.7 %all-gather.6.cloned.1.call-start = ((), (), s32[]{:S(2)}) async-start(), calls=%async_computation.4 | async-start | bytes 3993600 | tf_op jit(solution)/shard_map/all_gather | solution.py:30
  8.1 15.8 %collective-permute-start = (bf16[1024,320]{0,1:T(8,128)(2,1)}, bf16[1024,320]{0,1:T(8,128)(2,1)S(1)}, u32[]{:S(2)}, u32[]{:S(2)}) collective-permute-start(bf16[1024,320]{0,1:T(8,128)(2,1)} %param.11), channel_id=1, source_target_pairs={{0,1},{1,2},{2,3},{3,0},{4,5},{5,6},{6,7},{7,4},{8,9},{9,10},{10,1... | collective-permute-start | bytes 1966088 | tf_op jit(solution)/shard_map/ppermute | solution.py:11
  23.8 15.4 %collective-permute-start.1 = (bf16[1024,320]{0,1:T(8,128)(2,1)S(1)}, bf16[1024,320]{0,1:T(8,128)(2,1)S(1)}, u32[]{:S(2)}, u32[]{:S(2)}) collective-permute-start(bf16[1024,320]{0,1:T(8,128)(2,1)S(1)} %collective-permute-done), channel_id=1, source_target_pairs={{0,1},{1,2},{2,3},{3,0},{4,5},{5,6},{6,7},{7,4},{8,9},{9,10},{10,1... | collective-permute-start | bytes 1966088 | tf_op jit(solution)/shard_map/ppermute | solution.py:11
  39.2 14.0 %collective-permute-start.2 = (bf16[1024,320]{0,1:T(8,128)(2,1)S(1)}, bf16[1024,320]{0,1:T(8,128)(2,1)S(1)}, u32[]{:S(2)}, u32[]{:S(2)}) collective-permute-start(bf16[1024,320]{0,1:T(8,128)(2,1)S(1)} %collective-permute-done.1), channel_id=1, source_target_pairs={{0,1},{1,2},{2,3},{3,0},{4,5},{5,6},{6,7},{7,4},{8,9},{9,10},{10,1... | collective-permute-start | bytes 1966088 | tf_op jit(solution)/shard_map/ppermute | solution.py:11
  40.2 246.2 %reduce-scatter.3.cloned.1.call-start = ((), (), s32[]{:S(2)}) async-start(), calls=%async_computation.3 | async-start | bytes 3276800 | tf_op jit(solution)/shard_map/reduce_scatter | solution.py:35
  54.7 2.3 copy-start
  99.3 78.8 %copy-start.9 = (f32[1280]{0:T(1024)S(1)}, f32[1280]{0:T(1024)}, u32[]{:S(2)}) copy-start(f32[1280]{0:T(1024)} %param.15) | copy-start | bytes 15364
  99.3 78.8 %copy-start.10 = (f32[1280]{0:T(1024)S(1)}, f32[1280]{0:T(1024)}, u32[]{:S(2)}) copy-start(f32[1280]{0:T(1024)} %param.13) | copy-start | bytes 15364
  99.3 78.8 %copy-start.11 = (f32[1280]{0:T(1024)S(1)}, f32[1280]{0:T(1024)}, u32[]{:S(2)}) copy-start(f32[1280]{0:T(1024)} %param.12) | copy-start | bytes 15364
  178.1 22.3 %copy-start.2 = (s32[16384]{0:T(1024)S(1)}, s32[16384]{0:T(1024)}, u32[]{:S(2)}) copy-start(s32[16384]{0:T(1024)} %param.21) | copy-start | bytes 196612
  200.3 86.1 %copy-start.5 = (f32[320]{0:T(512)S(1)}, f32[320]{0:T(512)}, u32[]{:S(2)}) copy-start(f32[320]{0:T(512)} %param.17) | copy-start | bytes 3844
  200.3 115.8 %reduce-scatter.5.cloned.1.call-start = ((), (), s32[]{:S(2)}) async-start(), calls=%async_computation.5 | async-start | bytes 819200 | tf_op jit(solution)/shard_map/reduce_scatter | solution.py:67
  201.4 86.7 %copy-start.4 = (s32[64,3]{0,1:T(4,128)}, s32[64,3]{0,1:T(4,128)S(1)}, u32[]{:S(2)}) copy-start(s32[64,3]{0,1:T(4,128)S(1)} %reduce-window.19) | copy-start | bytes 2308
  287.8 28.4 %copy-start.6 = (f32[320]{0:T(512)S(1)}, f32[320]{0:T(512)}, u32[]{:S(2)}) copy-start(f32[320]{0:T(512)} %param.19) | copy-start | bytes 3844
  288.9 5.3 %slice-start = ((s32[64,3]{0,1:T(4,128)}), s32[64,2]{0,1:T(2,128)S(1)}, s32[]{:S(2)}) async-start(s32[64,3]{0,1:T(4,128)} %copy-done.4), calls=%async_computation.8 | async-start | bytes 2048 | tf_op jit(solution)/shard_map/slice.3
  288.9 72.0 %copy-start.8 = (s32[2]{0:T(128)S(1)}, s32[2]{0:T(128)}, u32[]{:S(2)}) copy-start(s32[2]{0:T(128)} %constant.161) | copy-start | bytes 28
  288.9 72.1 %copy-start.7 = (s32[2]{0:T(128)S(1)}, s32[2]{0:T(128)}, u32[]{:S(2)}) copy-start(s32[2]{0:T(128)} %constant.164) | copy-start | bytes 28
  293.1 128.7 %copy-start.3 = (bf16[512,320]{0,1:T(8,128)(2,1)S(1)}, bf16[512,320]{0,1:T(8,128)(2,1)}, u32[]{:S(2)}) copy-start(bf16[512,320]{0,1:T(8,128)(2,1)} %param.20) | copy-start | bytes 983044
  349.0 73.0 %all-to-all-start = ((bf16[64,8,320]{2,1,0:T(8,128)(2,1)}), bf16[64,8,320]{2,1,0:T(8,128)(2,1)S(1)}, u32[]{:S(2)}, u32[]{:S(2)}) async-start(bf16[64,8,320]{2,1,0:T(8,128)(2,1)} %scatter_fusion), calls=%async_computation.2 | async-start | bytes 786432 | tf_op jit(solution)/shard_map/all_to_all | solution.py:73
Sparse Core Ops, SparseCore 0:
  10.0 83.1 all-gather.7
  95.9 76.0 all-gather.9
  174.7 76.0 all-gather.5
  253.1 33.2 reduce-scatter.2
  293.2 22.8 reduce-scatter.4
